TPU v7x, 32 devices: a whole 2x2x4 slice. The times are simulated.
32 devices in a mesh: sub: 8 (over y, x, core), reg: 4 (over z).
Axes of the slice: x: 2, y: 2, z: 4, core: 2. Of those that a mesh axis runs over, the one named last changes fastest.
Arguments:
- right_side: float32 [8, 4, 1280, 16], P('sub', 'reg'), may hold values from -6 to 6
- tiles: bfloat16 [8, 4, 80, 128, 128], P('sub', 'reg'), may hold values from -1 to 5
- tile_list: int32 [8, 4, 80, 2], P('sub', 'reg'), may hold values from 0 to 9, as said below
- weights: float32 [8, 4, 1280], P('sub', 'reg'), may hold values from 0.15 to 0.35
- face_map: int32 [8, 4, 6], P('sub', 'reg'), may hold values from 0 to 9, as said below
- matching: int32 [8, 4, 6, 128], P('sub', 'reg'), may hold values from 0 to 127, each once within a row
- coarse_basis: bfloat16 [8, 4, 1280, 128], P('sub', 'reg'), may hold values from -0.15625 to 0.15625
- coarse_map: int32 [8, 4, 128], P('sub', 'reg'), may hold values from 0 to 511, as said below
- coarse_inverse: float32 [4, 512, 512], P('reg', 'sub'), may hold values from -1 to 2, as said below
Outputs:
- solution: bfloat16 [8, 4, 1280, 16], P('sub', 'reg')
- residual: bfloat16 [8, 4, 1280, 16], P('sub', 'reg')
Inputs may be any that keep to these rules, and one draw needn't show every extreme that they name: `tile_list`: entries 0 to 9 of each subdomain's list are (b, b) for b in order; the other 70 entries are distinct off-diagonal block pairs. `face_map`: the six blocks of a subdomain are distinct. `coarse_map`: A subdomain's 128 numbers are distinct, and within a subregion every number is named by exactly two subdomains. `coarse_inverse`: symmetric in its last two dimensions.
All inputs are finite; a program needn't handle non-finite values.
Results may differ from a plain program's by a relative error of at most 0.0075.
Values may be sent and summed in bfloat16 or wider, within the bound.
No kernel may reach another device: no remote copies, remote signals or barrier semaphores. Data moves between devices by JAX's collectives and lax.ppermute only.
A program may use at most 64 MiB of HBM per device.

v0:
```python
import jax
import jax.numpy as jnp
from jax import lax
from jax.sharding import PartitionSpec as P

SWEEPS = 3


def from_behind(shard, axis, by):
    peers = lax.axis_size(axis)
    return lax.ppermute(shard, axis, [(i, (i + by) % peers) for i in range(peers)])


def body(
    right_side,
    tiles,
    tile_list,
    weights,
    face_map,
    matching,
    coarse_basis,
    coarse_map,
    coarse_inverse,
):
    order = right_side.shape[2]
    rights = right_side.shape[3]
    tile = tiles.shape[3]
    blocks = order // tile
    target = right_side[0, 0]
    tile_block = tiles[0, 0]
    listing = tile_list[0, 0]
    scaling = weights[0, 0][:, None]
    faces_here = face_map[0, 0]
    matched = matching[0, 0]
    basis = coarse_basis[0, 0]
    own_map = coarse_map[0, 0]
    own_count = own_map.shape[0]
    inverse_rows = coarse_inverse[0]
    held_rows = inverse_rows.shape[0]
    block_ids = jnp.arange(blocks, dtype=jnp.int32)
    row_table = (listing[:, 0][None, :] == block_ids[:, None]).astype(jnp.float32)
    face_table = (faces_here[None, :] == block_ids[:, None]).astype(jnp.float32)
    stride = max(lax.axis_size("reg") // 4, 1)
    every_ids = lax.all_gather(own_map, "sub", axis=0, tiled=True)
    outgoing_part = jnp.take(inverse_rows, every_ids, axis=1).reshape(
        held_rows, lax.axis_size("sub"), own_count
    )
    received_part = lax.all_to_all(outgoing_part, "sub", split_axis=1, concat_axis=0, tiled=True)
    own_columns = received_part.reshape(held_rows * lax.axis_size("sub"), own_count)
    own_block = jnp.transpose(jnp.take(own_columns, every_ids, axis=0))
    solution = jnp.zeros_like(target)
    residual = target
    for sweep in range(SWEEPS):
        low = residual.astype(jnp.bfloat16)
        local_coarse = jnp.einsum("mn,mr->nr", basis, low, preferred_element_type=jnp.float32)
        own_solution = jnp.dot(
            own_block,
            lax.all_gather(local_coarse, "sub", axis=0, tiled=True),
            precision=lax.Precision.HIGHEST,
            preferred_element_type=jnp.float32,
        )
        own_values = own_solution.astype(jnp.bfloat16)
        correction = jnp.dot(basis, own_values, preferred_element_type=jnp.float32)
        solution = solution + (scaling * residual + correction)
        operator_low = solution.astype(jnp.bfloat16).reshape(blocks, tile, rights)
        picked = jnp.take(operator_low, listing[:, 1], axis=0)
        products = jnp.einsum(
            "tij,tjr->tir", tile_block, picked, preferred_element_type=jnp.float32
        )
        local = jnp.einsum("bt,tir->bir", row_table, products, precision=lax.Precision.HIGHEST)
        stacked = solution.reshape(blocks, tile, rights)
        outgoing = jnp.take(stacked, faces_here, axis=0)
        arrived = []
        for face, offset in ((0, 1), (1, -1), (2, stride), (3, -stride)):
            arrived.append(from_behind(outgoing[face ^ 1], "reg", offset))
        for face, offset in ((4, 1), (5, -1)):
            arrived.append(from_behind(outgoing[face ^ 1], "sub", offset))
        received = jnp.stack(arrived)
        permuted = jnp.take_along_axis(received, matched[:, :, None], axis=1)
        coupling = jnp.einsum("bk,kir->bir", face_table, permuted, precision=lax.Precision.HIGHEST)
        residual = target - (local - 0.5 * coupling).reshape(order, rights)
    shape = (1, 1, order, rights)
    return (
        solution.astype(jnp.bfloat16).reshape(shape),
        residual.astype(jnp.bfloat16).reshape(shape),
    )


def solution(mesh):
    placed = (
        P("sub", "reg", None, None),
        P("sub", "reg", None, None, None),
        P("sub", "reg", None, None),
        P("sub", "reg", None),
        P("sub", "reg", None),
        P("sub", "reg", None, None),
        P("sub", "reg", None, None),
        P("sub", "reg", None),
        P("reg", "sub", None),
    )
    return jax.shard_map(
        body,
        mesh=mesh,
        in_specs=placed,
        out_specs=(P("sub", "reg", None, None), P("sub", "reg", None, None)),
        check_vma=False,
    )
```

profile of v0, /device:TPU:0, one launch (start us, length us, event | category | flops | bytes accessed | tf_op | source)
XLA Modules:
  0.0 149.0 jit_solution(13466135424913627133)
XLA Ops:
  0.7 10.7 %all-gather = s32[1,1,1024]{2,1,0:T(1,128)S(1)} all-gather(s32[1,1,128]{2,1,0:T(1,128)} %param.22), channel_id=2, replica_groups=mesh['sub'=8,'reg'=4] {'sub'}, dimensions={2}, use_global_device_ids=true | all-gather | bytes 4608 | tf_op jit(solution)/shard_map/all_gather | solution.py:44
  11.4 1.0 copy.30
  12.4 4.0 %gather_fusion = f32[1024,64]{1,0:T(8,128)} fusion(f32[64,512]{0,1:T(8,128)S(1)} %bitcast.251, s32[1024]{0:T(1024)S(1)} %fusion.82), kind=kCustom, calls=%fused_computation.9 | custom fusion | bytes 528384 | tf_op jit(solution)/shard_map/jit(_take)/gather | solution.py:45
  16.4 1.2 copy.31
  17.6 0.7 broadcast_select_fusion
  18.3 3.4 %all-to-all-start = ((f32[64,8,128]{2,0,1:T(8,128)}), f32[64,8,128]{2,0,1:T(8,128)S(1)}, u32[]{:S(2)}, u32[]{:S(2)}) async-start(f32[64,8,128]{2,0,1:T(8,128)} %broadcast_select_fusion), calls=%async_computation | async-start | bytes 524288 | tf_op jit(solution)/shard_map/all_to_all | solution.py:48
  23.7 9.5 %all_gather.13 = f32[1024,16]{0,1:T(8,128)S(1)} all-gather(f32[128,16]{0,1:T(8,128)S(1)} %fusion.37), channel_id=1, replica_groups=mesh['sub'=8,'reg'=4] {'sub'}, dimensions={0}, use_global_device_ids=true | all-gather | bytes 73728 | tf_op jit(solution)/shard_map/all_gather | solution.py:58
  33.3 4.0 %gather_fusion.1 = f32[1024,128]{1,0:T(8,128)} fusion(f32[512,128]{1,0:T(8,128)S(1)} %bitcast.250, s32[1024]{0:T(1024)S(1)} %fusion.82), kind=kCustom, calls=%fused_computation.10 | custom fusion | bytes 1052672 | tf_op jit(solution)/shard_map/jit(_take)/gather | solution.py:50
  37.2 1.5 %convolution_convert_fusion.2 = bf16[128,16]{0,1:T(8,128)(2,1)S(1)} fusion(f32[1024,16]{0,1:T(8,128)S(1)} %all_gather.13, f32[1024,128]{1,0:T(8,128)} %gather_fusion.1, pred[1024]{0:T(1024)(128)(4,1)S(1)} %compare_and_fusion.1), kind=kOutput, calls=%fused_computation.38 | convolution fusion | flops 25298944 | bytes 594944 | tf_op jit(solution)/shard_map/dot_general | solution.py:56
  39.7 1.6 %collective-permute-start = (f32[128,16]{0,1:T(8,128)S(1)}, f32[128,16]{0,1:T(8,128)}, u32[]{:S(2)}, u32[]{:S(2)}) collective-permute-start(f32[128,16]{0,1:T(8,128)S(1)} %get-tuple-element.26), channel_id=1, source_target_pairs={{0,1},{1,2},{2,3},{3,0},{4,5},{5,6},{6,7},{7,4},{8,9},{9,10},{10,1... | collective-permute-start | bytes 24584 | tf_op jit(solution)/shard_map/ppermute | solution.py:11
  41.3 2.2 %collective-permute-start.1 = (f32[128,16]{0,1:T(8,128)S(1)}, f32[128,16]{0,1:T(8,128)}, u32[]{:S(2)}, u32[]{:S(2)}) collective-permute-start(f32[128,16]{0,1:T(8,128)S(1)} %get-tuple-element.25), channel_id=1, source_target_pairs={{0,3},{1,0},{2,1},{3,2},{4,7},{5,4},{6,5},{7,6},{8,11},{9,8},{10,9... | collective-permute-start | bytes 24584 | tf_op jit(solution)/shard_map/ppermute | solution.py:11
  43.6 3.8 %collective-permute-start.3 = (f32[128,16]{0,1:T(8,128)S(1)}, f32[128,16]{0,1:T(8,128)}, u32[]{:S(2)}, u32[]{:S(2)}) collective-permute-start(f32[128,16]{0,1:T(8,128)S(1)} %get-tuple-element.23), channel_id=1, source_target_pairs={{0,3},{1,0},{2,1},{3,2},{4,7},{5,4},{6,5},{7,6},{8,11},{9,8},{10,9... | collective-permute-start | bytes 24584 | tf_op jit(solution)/shard_map/ppermute | solution.py:11
  47.4 0.8 gather_fusion.2
  48.2 2.2 %fusion.11 = f32[80,128,16]{1,2,0:T(8,128)S(1)} fusion(bf16[1,1,80,128,128]{4,3,2,1,0:T(8,128)(2,1)S(1)} %copy-done, bf16[80,128,16]{1,2,0:T(8,128)(2,1)S(1)} %gather_fusion.2, pred[80]{0:T(512)(128)(4,1)} %get-tuple-element.4), kind=kOutput, calls=%fused_computation.25 | convolution fusion | flops 42106880 | bytes 3604560 | tf_op jit(solution)/shard_map/tij,tjr->tir/dot_general | solution.py:67
  50.3 1.2 fusion.27
  51.5 2.6 %collective-permute-start.5 = (f32[128,16]{0,1:T(8,128)S(1)}, f32[128,16]{0,1:T(8,128)S(1)}, u32[]{:S(2)}, u32[]{:S(2)}) collective-permute-start(f32[128,16]{0,1:T(8,128)S(1)} %get-tuple-element.21), channel_id=1, source_target_pairs={{0,28},{4,0},{8,4},{12,8},{16,12},{20,16},{24,20},{28,24},{1,29},{... | collective-permute-start | bytes 24584 | tf_op jit(solution)/shard_map/ppermute | solution.py:11
  54.2 1.3 constant_dynamic-update-slice_fusion.5
  55.5 1.3 constant_dynamic-update-slice_fusion.4
  56.8 1.3 constant_dynamic-update-slice_fusion.3
  58.1 1.3 constant_dynamic-update-slice_fusion.2
  59.4 1.3 constant_dynamic-update-slice_fusion.1
  61.3 1.0 copy.35
  62.2 7.0 %gather_fusion.4 = f32[768,16]{1,0:T(8,128)} fusion(f32[6,128,16]{2,1,0:T(8,128)S(1)} %copy.35, s32[768]{0:T(1024)S(1)} %bitcast.246), kind=kCustom, calls=%fused_computation.2.clone | custom fusion | bytes 104448 | tf_op jit(solution)/shard_map/jit(take_along_axis)/gather | solution.py:79
  69.2 1.2 copy.36
  70.4 1.2 fusion.22
  71.8 9.0 %all_gather.14 = f32[1024,16]{0,1:T(8,128)S(1)} all-gather(f32[128,16]{0,1:T(8,128)S(1)} %convolution_bitcast_fusion.4), channel_id=1, replica_groups=mesh['sub'=8,'reg'=4] {'sub'}, dimensions={0}, use_global_device_ids=true | all-gather | bytes 73728 | tf_op jit(solution)/shard_map/all_gather | solution.py:58
  80.8 1.5 %convolution_convert_fusion.1 = bf16[128,16]{0,1:T(8,128)(2,1)S(1)} fusion(f32[1024,16]{0,1:T(8,128)S(1)} %all_gather.14, f32[1024,128]{1,0:T(8,128)} %gather_fusion.1, pred[1024]{0:T(1024)(128)(4,1)S(1)} %compare_and_fusion.1), kind=kOutput, calls=%fused_computation.37 | convolution fusion | flops 25298944 | bytes 594944 | tf_op jit(solution)/shard_map/dot_general | solution.py:56
  83.2 0.9 gather_fusion.5
  84.2 2.4 %fusion.14 = f32[80,128,16]{1,2,0:T(8,128)} fusion(bf16[1,1,80,128,128]{4,3,2,1,0:T(8,128)(2,1)S(1)} %copy-done, bf16[80,128,16]{1,2,0:T(8,128)(2,1)S(1)} %gather_fusion.5, pred[80]{0:T(512)(128)(4,1)S(1)} %copy-done.13), kind=kOutput, calls=%fused_computation.26 | convolution fusion | flops 42106880 | bytes 3604560 | tf_op jit(solution)/shard_map/tij,tjr->tir/dot_general | solution.py:67
  87.3 2.2 %fusion.25 = f32[10,128,16]{1,0,2:T(8,128)} fusion(f32[80,128,16]{1,2,0:T(8,128)} %fusion.14, s32[80]{0:T(128)S(1)} %copy-done.12), kind=kOutput, calls=%fused_computation.41 | convolution fusion | flops 19661600 | bytes 737600 | tf_op jit(solution)/shard_map/bt,tir->bir/dot_general | solution.py:70
  89.5 3.8 %collective-permute-start.7 = (f32[128,16]{0,1:T(8,128)S(1)}, f32[128,16]{0,1:T(8,128)S(1)}, u32[]{:S(2)}, u32[]{:S(2)}) collective-permute-start(f32[128,16]{0,1:T(8,128)S(1)} %get-tuple-element.19), channel_id=1, source_target_pairs={{0,3},{1,0},{2,1},{3,2},{4,7},{5,4},{6,5},{7,6},{8,11},{9,8},{10,9... | collective-permute-start | bytes 24584 | tf_op jit(solution)/shard_map/ppermute | solution.py:11
  93.3 3.8 %collective-permute-start.9 = (f32[128,16]{0,1:T(8,128)S(1)}, f32[128,16]{0,1:T(8,128)S(1)}, u32[]{:S(2)}, u32[]{:S(2)}) collective-permute-start(f32[128,16]{0,1:T(8,128)S(1)} %get-tuple-element.17), channel_id=1, source_target_pairs={{0,3},{1,0},{2,1},{3,2},{4,7},{5,4},{6,5},{7,6},{8,11},{9,8},{10,9... | collective-permute-start | bytes 24584 | tf_op jit(solution)/shard_map/ppermute | solution.py:11
  97.1 2.6 %collective-permute-start.11 = (f32[128,16]{0,1:T(8,128)S(1)}, f32[128,16]{0,1:T(8,128)S(1)}, u32[]{:S(2)}, u32[]{:S(2)}) collective-permute-start(f32[128,16]{0,1:T(8,128)S(1)} %get-tuple-element.15), channel_id=1, source_target_pairs={{0,28},{4,0},{8,4},{12,8},{16,12},{20,16},{24,20},{28,24},{1,29},{... | collective-permute-start | bytes 24584 | tf_op jit(solution)/shard_map/ppermute | solution.py:11
  99.8 1.3 collective-permute-done.10
  101.3 7.0 %gather_fusion.7 = f32[768,16]{1,0:T(8,128)} fusion(f32[6,128,16]{2,1,0:T(8,128)S(1)} %copy.40, s32[768]{0:T(1024)S(1)} %bitcast.247), kind=kCustom, calls=%fused_computation.7.clone | custom fusion | bytes 104448 | tf_op jit(solution)/shard_map/jit(take_along_axis)/gather | solution.py:79
  108.3 1.2 copy.41
  109.5 1.2 fusion.21
  110.9 9.3 %all_gather.15 = f32[1024,16]{0,1:T(8,128)S(1)} all-gather(f32[128,16]{0,1:T(8,128)S(1)} %convolution_bitcast_fusion.3), channel_id=1, replica_groups=mesh['sub'=8,'reg'=4] {'sub'}, dimensions={0}, use_global_device_ids=true | all-gather | bytes 73728 | tf_op jit(solution)/shard_map/all_gather | solution.py:58
  120.2 1.5 %convolution_convert_fusion = bf16[128,16]{0,1:T(8,128)(2,1)S(1)} fusion(f32[1024,16]{0,1:T(8,128)S(1)} %all_gather.15, f32[1024,128]{1,0:T(8,128)} %gather_fusion.1, pred[1024]{0:T(1024)(128)(4,1)S(1)} %compare_and_fusion.1), kind=kOutput, calls=%fused_computation.36 | convolution fusion | flops 25298944 | bytes 594944 | tf_op jit(solution)/shard_map/dot_general | solution.py:56
  122.6 0.8 gather_fusion.8
  123.4 2.4 %fusion.17 = f32[80,128,16]{1,2,0:T(8,128)} fusion(bf16[1,1,80,128,128]{4,3,2,1,0:T(8,128)(2,1)S(1)} %copy-done, bf16[80,128,16]{1,2,0:T(8,128)(2,1)S(1)} %gather_fusion.8, pred[80]{0:T(512)(128)(4,1)S(1)} %copy-done.13), kind=kOutput, calls=%fused_computation.27 | convolution fusion | flops 42106880 | bytes 3604560 | tf_op jit(solution)/shard_map/tij,tjr->tir/dot_general | solution.py:67
  126.4 1.6 %fusion.23 = f32[10,128,16]{1,0,2:T(8,128)S(1)} fusion(f32[80,128,16]{1,2,0:T(8,128)} %fusion.17, s32[80]{0:T(128)S(1)} %copy-done.12), kind=kOutput, calls=%fused_computation.39 | convolution fusion | flops 19661600 | bytes 737600 | tf_op jit(solution)/shard_map/bt,tir->bir/dot_general | solution.py:70
  128.0 3.9 %collective-permute-start.13 = (f32[128,16]{0,1:T(8,128)S(1)}, f32[128,16]{0,1:T(8,128)S(1)}, u32[]{:S(2)}, u32[]{:S(2)}) collective-permute-start(f32[128,16]{0,1:T(8,128)S(1)} %get-tuple-element.13), channel_id=1, source_target_pairs={{0,3},{1,0},{2,1},{3,2},{4,7},{5,4},{6,5},{7,6},{8,11},{9,8},{10,9... | collective-permute-start | bytes 24584 | tf_op jit(solution)/shard_map/ppermute | solution.py:11
  131.9 3.8 %collective-permute-start.15 = (f32[128,16]{0,1:T(8,128)S(1)}, f32[128,16]{0,1:T(8,128)S(1)}, u32[]{:S(2)}, u32[]{:S(2)}) collective-permute-start(f32[128,16]{0,1:T(8,128)S(1)} %get-tuple-element.11), channel_id=1, source_target_pairs={{0,3},{1,0},{2,1},{3,2},{4,7},{5,4},{6,5},{7,6},{8,11},{9,8},{10,9... | collective-permute-start | bytes 24584 | tf_op jit(solution)/shard_map/ppermute | solution.py:11
  135.7 2.6 %collective-permute-start.17 = (f32[128,16]{0,1:T(8,128)S(1)}, f32[128,16]{0,1:T(8,128)S(1)}, u32[]{:S(2)}, u32[]{:S(2)}) collective-permute-start(f32[128,16]{0,1:T(8,128)S(1)} %get-tuple-element.9), channel_id=1, source_target_pairs={{0,28},{4,0},{8,4},{12,8},{16,12},{20,16},{24,20},{28,24},{1,29},{... | collective-permute-start | bytes 24584 | tf_op jit(solution)/shard_map/ppermute | solution.py:11
  138.4 1.3 collective-permute-done.16
  139.9 7.0 %gather_fusion.10 = f32[768,16]{1,0:T(8,128)} fusion(f32[6,128,16]{2,1,0:T(8,128)S(1)} %copy.45, s32[768]{0:T(1024)S(1)} %bitcast.248), kind=kCustom, calls=%fused_computation.8.clone | custom fusion | bytes 104448 | tf_op jit(solution)/shard_map/jit(take_along_axis)/gather | solution.py:79
  146.8 1.2 copy.46
  (109 shorter events, 8.4 us)
Async XLA Ops:
  0.6 47.6 %copy-start = (bf16[1,1,80,128,128]{4,3,2,1,0:T(8,128)(2,1)S(1)}, bf16[1,1,80,128,128]{4,3,2,1,0:T(8,128)(2,1)}, u32[]{:S(2)}) copy-start(bf16[1,1,80,128,128]{4,3,2,1,0:T(8,128)(2,1)} %param.16) | copy-start | bytes 7864324
  0.6 21.1 %copy-start.14 = (s32[1,1,80,2]{2,3,1,0:T(2,128)S(1)}, s32[1,1,80,2]{2,3,1,0:T(2,128)}, u32[]{:S(2)}) copy-start(s32[1,1,80,2]{2,3,1,0:T(2,128)} %param.17) | copy-start | bytes 1924
  0.7 22.2 %copy-start.7 = (s32[1,1,6]{2,1,0:T(1,128)S(1)}, s32[1,1,6]{2,1,0:T(1,128)}, u32[]{:S(2)}) copy-start(s32[1,1,6]{2,1,0:T(1,128)} %param.19) | copy-start | bytes 76
  0.7 22.2 %copy-start.5 = (s32[1,1,6,128]{3,1,2,0:T(1,128)S(1)}, s32[1,1,6,128]{3,1,2,0:T(1,128)}, u32[]{:S(2)}) copy-start(s32[1,1,6,128]{3,1,2,0:T(1,128)} %param.20) | copy-start | bytes 9220
  0.7 22.2 %copy-start.1 = (bf16[1,1,1280,128]{3,2,1,0:T(8,128)(2,1)S(1)}, bf16[1,1,1280,128]{3,2,1,0:T(8,128)(2,1)}, u32[]{:S(2)}) copy-start(bf16[1,1,1280,128]{3,2,1,0:T(8,128)(2,1)} %param.21) | copy-start | bytes 983044
  0.7 22.2 %copy-start.2 = (f32[1,1,1280,16]{2,3,1,0:T(8,128)S(1)}, f32[1,1,1280,16]{2,3,1,0:T(8,128)}, u32[]{:S(2)}) copy-start(f32[1,1,1280,16]{2,3,1,0:T(8,128)} %param.15) | copy-start | bytes 245764
  0.7 32.5 %copy-start.6 = (f32[1,1,1280]{2,1,0:T(1,128)S(1)}, f32[1,1,1280]{2,1,0:T(1,128)}, u32[]{:S(2)}) copy-start(f32[1,1,1280]{2,1,0:T(1,128)} %param.18) | copy-start | bytes 15364
  18.3 14.9 %all-to-all-start = ((f32[64,8,128]{2,0,1:T(8,128)}), f32[64,8,128]{2,0,1:T(8,128)S(1)}, u32[]{:S(2)}, u32[]{:S(2)}) async-start(f32[64,8,128]{2,0,1:T(8,128)} %broadcast_select_fusion), calls=%async_computation | async-start | bytes 524288 | tf_op jit(solution)/shard_map/all_to_all | solution.py:48
  22.9 16.7 %copy-start.9 = (pred[6]{0:T(512)(128)(4,1)}, pred[6]{0:T(512)(128)(4,1)S(1)}, u32[]{:S(2)}) copy-start(pred[6]{0:T(512)(128)(4,1)S(1)} %compare_and_fusion.2) | copy-start | bytes 22
  39.7 11.8 %collective-permute-start = (f32[128,16]{0,1:T(8,128)S(1)}, f32[128,16]{0,1:T(8,128)}, u32[]{:S(2)}, u32[]{:S(2)}) collective-permute-start(f32[128,16]{0,1:T(8,128)S(1)} %get-tuple-element.26), channel_id=1, source_target_pairs={{0,1},{1,2},{2,3},{3,0},{4,5},{5,6},{6,7},{7,4},{8,9},{9,10},{10,1... | collective-permute-start | bytes 24584 | tf_op jit(solution)/shard_map/ppermute | solution.py:11
  41.3 14.2 %collective-permute-start.1 = (f32[128,16]{0,1:T(8,128)S(1)}, f32[128,16]{0,1:T(8,128)}, u32[]{:S(2)}, u32[]{:S(2)}) collective-permute-start(f32[128,16]{0,1:T(8,128)S(1)} %get-tuple-element.25), channel_id=1, source_target_pairs={{0,3},{1,0},{2,1},{3,2},{4,7},{5,4},{6,5},{7,6},{8,11},{9,8},{10,9... | collective-permute-start | bytes 24584 | tf_op jit(solution)/shard_map/ppermute | solution.py:11
  43.6 13.2 %collective-permute-start.2 = (f32[128,16]{0,1:T(8,128)S(1)}, f32[128,16]{0,1:T(8,128)}, u32[]{:S(2)}, u32[]{:S(2)}) collective-permute-start(f32[128,16]{0,1:T(8,128)S(1)} %get-tuple-element.24), channel_id=1, source_target_pairs={{0,1},{1,2},{2,3},{3,0},{4,5},{5,6},{6,7},{7,4},{8,9},{9,10},{10,1... | collective-permute-start | bytes 24584 | tf_op jit(solution)/shard_map/ppermute | solution.py:11
  43.6 14.5 %collective-permute-start.3 = (f32[128,16]{0,1:T(8,128)S(1)}, f32[128,16]{0,1:T(8,128)}, u32[]{:S(2)}, u32[]{:S(2)}) collective-permute-start(f32[128,16]{0,1:T(8,128)S(1)} %get-tuple-element.23), channel_id=1, source_target_pairs={{0,3},{1,0},{2,1},{3,2},{4,7},{5,4},{6,5},{7,6},{8,11},{9,8},{10,9... | collective-permute-start | bytes 24584 | tf_op jit(solution)/shard_map/ppermute | solution.py:11
  47.4 12.0 %collective-permute-start.4 = (f32[128,16]{0,1:T(8,128)S(1)}, f32[128,16]{0,1:T(8,128)}, u32[]{:S(2)}, u32[]{:S(2)}) collective-permute-start(f32[128,16]{0,1:T(8,128)S(1)} %get-tuple-element.22), channel_id=1, source_target_pairs={{0,4},{4,8},{8,12},{12,16},{16,20},{20,24},{24,28},{28,0},{1,5},{5... | collective-permute-start | bytes 24584 | tf_op jit(solution)/shard_map/ppermute | solution.py:11
  48.2 2.2 %copy-start.11 = (s32[80]{0:T(128)S(1)}, s32[80]{0:T(128)}, u32[]{:S(2)}) copy-start(s32[80]{0:T(128)} %slice_bitcast_fusion.18) | copy-start | bytes 964
  51.5 18.8 %copy-start.8 = (s32[1,1,6]{2,1,0:T(1,128)S(1)}, s32[1,1,6]{2,1,0:T(1,128)}, u32[]{:S(2)}) copy-start(s32[1,1,6]{2,1,0:T(1,128)} %param.19) | copy-start | bytes 76
  51.5 9.1 %collective-permute-start.5 = (f32[128,16]{0,1:T(8,128)S(1)}, f32[128,16]{0,1:T(8,128)S(1)}, u32[]{:S(2)}, u32[]{:S(2)}) collective-permute-start(f32[128,16]{0,1:T(8,128)S(1)} %get-tuple-element.21), channel_id=1, source_target_pairs={{0,28},{4,0},{8,4},{12,8},{16,12},{20,16},{24,20},{28,24},{1,29},{... | collective-permute-start | bytes 24584 | tf_op jit(solution)/shard_map/ppermute | solution.py:11
  82.6 0.6 copy-start.3
  83.2 0.9 copy-start.13
  84.2 2.9 %copy-start.10 = (pred[6]{0:T(512)(128)(4,1)S(1)}, pred[6]{0:T(512)(128)(4,1)}, u32[]{:S(2)}) copy-start(pred[6]{0:T(512)(128)(4,1)} %copy-done.9) | copy-start | bytes 22
  84.2 3.1 %copy-start.12 = (s32[80]{0:T(128)S(1)}, s32[80]{0:T(128)}, u32[]{:S(2)}) copy-start(s32[80]{0:T(128)} %slice_bitcast_fusion.18) | copy-start | bytes 964
  87.2 9.9 %collective-permute-start.6 = (f32[128,16]{0,1:T(8,128)S(1)}, f32[128,16]{0,1:T(8,128)S(1)}, u32[]{:S(2)}, u32[]{:S(2)}) collective-permute-start(f32[128,16]{0,1:T(8,128)S(1)} %get-tuple-element.20), channel_id=1, source_target_pairs={{0,1},{1,2},{2,3},{3,0},{4,5},{5,6},{6,7},{7,4},{8,9},{9,10},{10,1... | collective-permute-start | bytes 24584 | tf_op jit(solution)/shard_map/ppermute | solution.py:11
  89.5 10.3 %collective-permute-start.7 = (f32[128,16]{0,1:T(8,128)S(1)}, f32[128,16]{0,1:T(8,128)S(1)}, u32[]{:S(2)}, u32[]{:S(2)}) collective-permute-start(f32[128,16]{0,1:T(8,128)S(1)} %get-tuple-element.19), channel_id=1, source_target_pairs={{0,3},{1,0},{2,1},{3,2},{4,7},{5,4},{6,5},{7,6},{8,11},{9,8},{10,9... | collective-permute-start | bytes 24584 | tf_op jit(solution)/shard_map/ppermute | solution.py:11
  93.3 6.5 %collective-permute-start.8 = (f32[128,16]{0,1:T(8,128)S(1)}, f32[128,16]{0,1:T(8,128)S(1)}, u32[]{:S(2)}, u32[]{:S(2)}) collective-permute-start(f32[128,16]{0,1:T(8,128)S(1)} %get-tuple-element.18), channel_id=1, source_target_pairs={{0,1},{1,2},{2,3},{3,0},{4,5},{5,6},{6,7},{7,4},{8,9},{9,10},{10,1... | collective-permute-start | bytes 24584 | tf_op jit(solution)/shard_map/ppermute | solution.py:11
  93.3 6.5 %collective-permute-start.9 = (f32[128,16]{0,1:T(8,128)S(1)}, f32[128,16]{0,1:T(8,128)S(1)}, u32[]{:S(2)}, u32[]{:S(2)}) collective-permute-start(f32[128,16]{0,1:T(8,128)S(1)} %get-tuple-element.17), channel_id=1, source_target_pairs={{0,3},{1,0},{2,1},{3,2},{4,7},{5,4},{6,5},{7,6},{8,11},{9,8},{10,9... | collective-permute-start | bytes 24584 | tf_op jit(solution)/shard_map/ppermute | solution.py:11
  97.1 4.0 %collective-permute-start.10 = (f32[128,16]{0,1:T(8,128)S(1)}, f32[128,16]{0,1:T(8,128)S(1)}, u32[]{:S(2)}, u32[]{:S(2)}) collective-permute-start(f32[128,16]{0,1:T(8,128)S(1)} %get-tuple-element.16), channel_id=1, source_target_pairs={{0,4},{4,8},{8,12},{12,16},{16,20},{20,24},{24,28},{28,0},{1,5},{5... | collective-permute-start | bytes 24584 | tf_op jit(solution)/shard_map/ppermute | solution.py:11
  97.1 4.0 %collective-permute-start.11 = (f32[128,16]{0,1:T(8,128)S(1)}, f32[128,16]{0,1:T(8,128)S(1)}, u32[]{:S(2)}, u32[]{:S(2)}) collective-permute-start(f32[128,16]{0,1:T(8,128)S(1)} %get-tuple-element.15), channel_id=1, source_target_pairs={{0,28},{4,0},{8,4},{12,8},{16,12},{20,16},{24,20},{28,24},{1,29},{... | collective-permute-start | bytes 24584 | tf_op jit(solution)/shard_map/ppermute | solution.py:11
  101.3 20.4 %copy-start.4 = (f32[1280,16]{0,1:T(8,128)S(1)}, f32[1280,16]{0,1:T(8,128)}, u32[]{:S(2)}) copy-start(f32[1280,16]{0,1:T(8,128)} %copy-done.3) | copy-start | bytes 245764
  126.4 9.3 %collective-permute-start.12 = (f32[128,16]{0,1:T(8,128)S(1)}, f32[128,16]{0,1:T(8,128)S(1)}, u32[]{:S(2)}, u32[]{:S(2)}) collective-permute-start(f32[128,16]{0,1:T(8,128)S(1)} %get-tuple-element.14), channel_id=1, source_target_pairs={{0,1},{1,2},{2,3},{3,0},{4,5},{5,6},{6,7},{7,4},{8,9},{9,10},{10,1... | collective-permute-start | bytes 24584 | tf_op jit(solution)/shard_map/ppermute | solution.py:11
  128.0 10.3 %collective-permute-start.13 = (f32[128,16]{0,1:T(8,128)S(1)}, f32[128,16]{0,1:T(8,128)S(1)}, u32[]{:S(2)}, u32[]{:S(2)}) collective-permute-start(f32[128,16]{0,1:T(8,128)S(1)} %get-tuple-element.13), channel_id=1, source_target_pairs={{0,3},{1,0},{2,1},{3,2},{4,7},{5,4},{6,5},{7,6},{8,11},{9,8},{10,9... | collective-permute-start | bytes 24584 | tf_op jit(solution)/shard_map/ppermute | solution.py:11
  131.9 6.5 %collective-permute-start.14 = (f32[128,16]{0,1:T(8,128)S(1)}, f32[128,16]{0,1:T(8,128)S(1)}, u32[]{:S(2)}, u32[]{:S(2)}) collective-permute-start(f32[128,16]{0,1:T(8,128)S(1)} %get-tuple-element.12), channel_id=1, source_target_pairs={{0,1},{1,2},{2,3},{3,0},{4,5},{5,6},{6,7},{7,4},{8,9},{9,10},{10,1... | collective-permute-start | bytes 24584 | tf_op jit(solution)/shard_map/ppermute | solution.py:11
  131.9 6.5 %collective-permute-start.15 = (f32[128,16]{0,1:T(8,128)S(1)}, f32[128,16]{0,1:T(8,128)S(1)}, u32[]{:S(2)}, u32[]{:S(2)}) collective-permute-start(f32[128,16]{0,1:T(8,128)S(1)} %get-tuple-element.11), channel_id=1, source_target_pairs={{0,3},{1,0},{2,1},{3,2},{4,7},{5,4},{6,5},{7,6},{8,11},{9,8},{10,9... | collective-permute-start | bytes 24584 | tf_op jit(solution)/shard_map/ppermute | solution.py:11
  135.7 4.0 %collective-permute-start.16 = (f32[128,16]{0,1:T(8,128)S(1)}, f32[128,16]{0,1:T(8,128)S(1)}, u32[]{:S(2)}, u32[]{:S(2)}) collective-permute-start(f32[128,16]{0,1:T(8,128)S(1)} %get-tuple-element.10), channel_id=1, source_target_pairs={{0,4},{4,8},{8,12},{12,16},{16,20},{20,24},{24,28},{28,0},{1,5},{5... | collective-permute-start | bytes 24584 | tf_op jit(solution)/shard_map/ppermute | solution.py:11
  135.7 4.0 %collective-permute-start.17 = (f32[128,16]{0,1:T(8,128)S(1)}, f32[128,16]{0,1:T(8,128)S(1)}, u32[]{:S(2)}, u32[]{:S(2)}) collective-permute-start(f32[128,16]{0,1:T(8,128)S(1)} %get-tuple-element.9), channel_id=1, source_target_pairs={{0,28},{4,0},{8,4},{12,8},{16,12},{20,16},{24,20},{28,24},{1,29},{... | collective-permute-start | bytes 24584 | tf_op jit(solution)/shard_map/ppermute | solution.py:11
where the time goes:
time: 150 us; the launch traced here: 149 us
  local copies, waits for them, and re-layouts  48.4 us (32%)
  blocking collectives  38.5 us (26%)
  starting transfers between devices  34.5 us (23%)
  matrix products  20.4 us (14%)
  other arithmetic  3.46 us (2%)
  waiting for transfers between devices  2.68 us (2%)
    ppermute x18, starting transfers between devices, from_behind(): lax.ppermute(shard, axis, [(i, (i + by) % peers) for i in range(peers)])  31.1 us
    all_gather x3, blocking collectives, body(): lax.all_gather(local_coarse, 'sub', axis=0, tiled=True)  27.8 us
    gather x6, local copies, waits for them, and re-layouts, body(): permuted = jnp.take_along_axis(received, matched[:, :, None], axis=1)  24.4 us
    all_gather x1, blocking collectives, body(): every_ids = lax.all_gather(own_map, 'sub', axis=0, tiled=True)  10.7 us
    unnamed x47, local copies, waits for them, and re-layouts  8.21 us
    dot_general x3, matrix products, body(): jnp.einsum('tij,tjr->tir', tile_block, picked, preferred_element_type=jnp...  6.87 us
    gather x2, local copies, waits for them, and re-layouts, body(): jnp.take(inverse_rows, every_ids, axis=1)  5.21 us
    dot_general x3, matrix products, body(): jnp.einsum('bt,tir->bir', row_table, products, precision=lax.Precision.HI...  4.98 us
  transfers between devices with their start and end apart: 19, of which 2 were waited for; matrix products, arithmetic and copies ran while one was open for 11% of the time, Pallas kernels for 0%

commit v1 on v0

--- a/solution.py
+++ b/solution.py
@@ -41,7 +41,15 @@
     row_table = (listing[:, 0][None, :] == block_ids[:, None]).astype(jnp.float32)
     face_table = (faces_here[None, :] == block_ids[:, None]).astype(jnp.float32)
     stride = max(lax.axis_size("reg") // 4, 1)
-    every_ids = lax.all_gather(own_map, "sub", axis=0, tiled=True)
+    ways, here = (lax.axis_size("sub"), lax.axis_index("sub"))
+    grown, reach = (own_map, 1)
+    while reach < ways:
+        theirs = lax.ppermute(grown, "sub", [(d, d ^ reach) for d in range(ways)])
+        mine_first = jnp.concatenate([grown, theirs], axis=0)
+        theirs_first = jnp.concatenate([theirs, grown], axis=0)
+        grown = jnp.where(here & reach == 0, mine_first, theirs_first)
+        reach = 2 * reach
+    every_ids = grown
     outgoing_part = jnp.take(inverse_rows, every_ids, axis=1).reshape(
         held_rows, lax.axis_size("sub"), own_count
     )

time: 150 us -> 149 us (level)
  blocking collectives: 38.5 us -> 27.9 us
  starting transfers between devices: 34.5 us -> 40.2 us
  local copies, waits for them, and re-layouts: 48.4 us -> 44.1 us
  other arithmetic: 3.46 us -> 6.98 us
  matrix products: 20.4 us -> 23 us
  waiting for transfers between devices: 2.68 us -> 4.38 us
    all_gather x1 -> x0, blocking collectives: 10.7 us -> none  [body(): every_ids = lax.all_gather(own_map, 'sub', axis=0, tiled=True)]
    ppermute x0 -> x3, starting transfers between devices: none -> 5.08 us  [body(): theirs = lax.ppermute(grown, 'sub', [(d, d ^ reach) for d in range(ways)])]
    gather x6, local copies, waits for them, and re-layouts: 24.4 us -> 21.6 us  [body(): permuted = jnp.take_along_axis(received, matched[:, :, None], axis=1)]
    gather x2, local copies, waits for them, and re-layouts: 5.21 us -> 2.99 us  [body(): jnp.take(inverse_rows, every_ids, axis=1)]
    ppermute x0 -> x3, waiting for transfers between devices: none -> 1.7 us  [body(): theirs = lax.ppermute(grown, 'sub', [(d, d ^ reach) for d in range(ways)])]
    unnamed x47 -> x43, local copies, waits for them, and re-layouts: 8.21 us -> 8.19 us
  transfers between devices with their start and end apart: 19 -> 22, of which waited for: 2 -> 3; matrix products, arithmetic and copies ran while one was open for 11% -> 15% of each run, Pallas kernels for 0% -> 0%
where the time goes in v1:
time: 149 us; the launch traced here: 148 us
  local copies, waits for them, and re-layouts  44.1 us (30%)
  starting transfers between devices  40.2 us (27%)
  blocking collectives  27.9 us (19%)
  matrix products  23 us (15%)
  other arithmetic  6.98 us (5%)
  waiting for transfers between devices  4.38 us (3%)
    ppermute x18, starting transfers between devices, from_behind(): lax.ppermute(shard, axis, [(i, (i + by) % peers) for i in range(peers)])  31 us
    all_gather x3, blocking collectives, body(): lax.all_gather(local_coarse, 'sub', axis=0, tiled=True)  27.9 us
    gather x6, local copies, waits for them, and re-layouts, body(): permuted = jnp.take_along_axis(received, matched[:, :, None], axis=1)  21.6 us
    unnamed x43, local copies, waits for them, and re-layouts  8.19 us
    dot_general x3, matrix products, body(): jnp.einsum('tij,tjr->tir', tile_block, picked, preferred_element_type=jnp...  6.9 us
    dot_general x3, matrix products, body(): jnp.einsum('bt,tir->bir', row_table, products, precision=lax.Precision.HI...  5.62 us
    ppermute x3, starting transfers between devices, body(): theirs = lax.ppermute(grown, 'sub', [(d, d ^ reach) for d in range(ways)])  5.08 us
    dot_general x3, matrix products, body(): jnp.dot(own_block, lax.all_gather(local_coarse, 'sub', axis=0, tiled=True...  4.59 us
  transfers between devices with their start and end apart: 22, of which 3 were waited for; matrix products, arithmetic and copies ran while one was open for 15% of the time, Pallas kernels for 0%

profile of v1, /device:TPU:0, one launch (start us, length us, event | category | flops | bytes accessed | tf_op | source)
XLA Modules:
  0.0 147.6 jit_solution(11925497378523238673)
XLA Ops:
  1.2 1.3 compare_and_fusion.4
  2.5 1.2 slice_bitcast_fusion.18
  5.7 1.2 fusion.37
  7.7 2.6 %collective-permute-start.1 = (s32[256]{0:T(256)S(1)}, s32[256]{0:T(256)S(1)}, u32[]{:S(2)}, u32[]{:S(2)}) collective-permute-start(s32[256]{0:T(256)S(1)} %add_select_fusion.4), channel_id=1, source_target_pairs={{0,8},{4,12},{8,0},{12,4},{16,24},{20,28},{24,16},{28,20},{1,9},{5... | collective-permute-start | bytes 3080 | tf_op jit(solution)/shard_map/ppermute | solution.py:47
  10.8 1.0 copy.30
  11.9 1.9 %collective-permute-start.2 = (s32[512]{0:T(512)S(1)}, s32[512]{0:T(512)S(1)}, u32[]{:S(2)}, u32[]{:S(2)}) collective-permute-start(s32[512]{0:T(512)S(1)} %add_select_fusion.2), channel_id=1, source_target_pairs={{0,16},{4,20},{8,24},{12,28},{16,0},{20,4},{24,8},{28,12},{1,17},{... | collective-permute-start | bytes 6152 | tf_op jit(solution)/shard_map/ppermute | solution.py:47
  13.9 1.7 %collective-permute-done.2 = s32[512]{0:T(512)S(1)} collective-permute-done((s32[512]{0:T(512)S(1)}, s32[512]{0:T(512)S(1)}, u32[]{:S(2)}, u32[]{:S(2)}) %collective-permute-start.2) | collective-permute-done | bytes 2080 | tf_op jit(solution)/shard_map/ppermute | solution.py:47
  15.6 2.8 %gather_fusion = f32[1024,64]{1,0:T(8,128)S(1)} fusion(f32[64,512]{0,1:T(8,128)S(1)} %bitcast.255, s32[1024]{0:T(1024)S(1)} %broadcast_clamp_fusion), kind=kCustom, calls=%fused_computation.9 | custom fusion | bytes 528384 | tf_op jit(solution)/shard_map/jit(_take)/gather | solution.py:53
  19.3 4.1 %all-to-all-start = ((f32[64,8,128]{2,0,1:T(8,128)}), f32[64,8,128]{2,0,1:T(8,128)S(1)}, u32[]{:S(2)}, u32[]{:S(2)}) async-start(f32[64,8,128]{2,0,1:T(8,128)} %broadcast_select_fusion), calls=%async_computation | async-start | bytes 524288 | tf_op jit(solution)/shard_map/all_to_all | solution.py:56
  23.4 10.3 %all_gather.9 = f32[1024,16]{0,1:T(8,128)S(1)} all-gather(f32[128,16]{0,1:T(8,128)S(1)} %fusion.37), channel_id=1, replica_groups=mesh['sub'=8,'reg'=4] {'sub'}, dimensions={0}, use_global_device_ids=true | all-gather | bytes 73728 | tf_op jit(solution)/shard_map/all_gather | solution.py:66
  33.8 4.0 %gather_fusion.1 = f32[1024,128]{1,0:T(8,128)} fusion(f32[512,128]{1,0:T(8,128)S(1)} %bitcast.254, s32[1024]{0:T(1024)S(1)} %broadcast_clamp_fusion), kind=kCustom, calls=%fused_computation.10 | custom fusion | bytes 1052672 | tf_op jit(solution)/shard_map/jit(_take)/gather | solution.py:58
  37.8 1.5 %convolution_convert_fusion.2 = bf16[128,16]{0,1:T(8,128)(2,1)S(1)} fusion(f32[1024,16]{0,1:T(8,128)S(1)} %all_gather.9, f32[1024,128]{1,0:T(8,128)} %gather_fusion.1, pred[1024]{0:T(1024)(128)(4,1)S(1)} %compare_and_fusion.2), kind=kOutput, calls=%fused_computation.38 | convolution fusion | flops 25298944 | bytes 594944 | tf_op jit(solution)/shard_map/dot_general | solution.py:64
  40.3 1.6 %collective-permute-start.3 = (f32[128,16]{0,1:T(8,128)S(1)}, f32[128,16]{0,1:T(8,128)}, u32[]{:S(2)}, u32[]{:S(2)}) collective-permute-start(f32[128,16]{0,1:T(8,128)S(1)} %get-tuple-element.26), channel_id=1, source_target_pairs={{0,1},{1,2},{2,3},{3,0},{4,5},{5,6},{6,7},{7,4},{8,9},{9,10},{10,1... | collective-permute-start | bytes 24584 | tf_op jit(solution)/shard_map/ppermute | solution.py:11
  41.9 2.2 %collective-permute-start.4 = (f32[128,16]{0,1:T(8,128)S(1)}, f32[128,16]{0,1:T(8,128)}, u32[]{:S(2)}, u32[]{:S(2)}) collective-permute-start(f32[128,16]{0,1:T(8,128)S(1)} %get-tuple-element.25), channel_id=1, source_target_pairs={{0,3},{1,0},{2,1},{3,2},{4,7},{5,4},{6,5},{7,6},{8,11},{9,8},{10,9... | collective-permute-start | bytes 24584 | tf_op jit(solution)/shard_map/ppermute | solution.py:11
  44.1 3.8 %collective-permute-start.6 = (f32[128,16]{0,1:T(8,128)S(1)}, f32[128,16]{0,1:T(8,128)}, u32[]{:S(2)}, u32[]{:S(2)}) collective-permute-start(f32[128,16]{0,1:T(8,128)S(1)} %get-tuple-element.23), channel_id=1, source_target_pairs={{0,3},{1,0},{2,1},{3,2},{4,7},{5,4},{6,5},{7,6},{8,11},{9,8},{10,9... | collective-permute-start | bytes 24584 | tf_op jit(solution)/shard_map/ppermute | solution.py:11
  48.8 2.2 %fusion.11 = f32[80,128,16]{1,2,0:T(8,128)S(1)} fusion(bf16[1,1,80,128,128]{4,3,2,1,0:T(8,128)(2,1)S(1)} %copy-done, bf16[80,128,16]{1,2,0:T(8,128)(2,1)S(1)} %gather_fusion.2, pred[80]{0:T(512)(128)(4,1)} %get-tuple-element.4), kind=kOutput, calls=%fused_computation.25 | convolution fusion | flops 42106880 | bytes 3604560 | tf_op jit(solution)/shard_map/tij,tjr->tir/dot_general | solution.py:75
  50.9 1.2 fusion.27
  52.1 2.6 %collective-permute-start.8 = (f32[128,16]{0,1:T(8,128)S(1)}, f32[128,16]{0,1:T(8,128)S(1)}, u32[]{:S(2)}, u32[]{:S(2)}) collective-permute-start(f32[128,16]{0,1:T(8,128)S(1)} %get-tuple-element.21), channel_id=1, source_target_pairs={{0,28},{4,0},{8,4},{12,8},{16,12},{20,16},{24,20},{28,24},{1,29},{... | collective-permute-start | bytes 24584 | tf_op jit(solution)/shard_map/ppermute | solution.py:11
  54.7 1.3 constant_dynamic-update-slice_fusion.5
  56.0 1.3 constant_dynamic-update-slice_fusion.4
  57.3 1.3 constant_dynamic-update-slice_fusion.3
  58.6 1.3 constant_dynamic-update-slice_fusion.2
  59.9 1.3 constant_dynamic-update-slice_fusion.1
  61.8 1.0 copy.35
  62.8 7.0 %gather_fusion.4 = f32[768,16]{1,0:T(8,128)} fusion(f32[6,128,16]{2,1,0:T(8,128)S(1)} %copy.35, s32[768]{0:T(1024)S(1)} %bitcast.250), kind=kCustom, calls=%fused_computation.2.clone | custom fusion | bytes 104448 | tf_op jit(solution)/shard_map/jit(take_along_axis)/gather | solution.py:87
  69.8 1.2 copy.36
  70.9 1.2 fusion.22
  72.4 8.4 %all_gather.10 = f32[1024,16]{0,1:T(8,128)S(1)} all-gather(f32[128,16]{0,1:T(8,128)S(1)} %convolution_bitcast_fusion.4), channel_id=1, replica_groups=mesh['sub'=8,'reg'=4] {'sub'}, dimensions={0}, use_global_device_ids=true | all-gather | bytes 73728 | tf_op jit(solution)/shard_map/all_gather | solution.py:66
  80.7 1.5 %convolution_convert_fusion.1 = bf16[128,16]{0,1:T(8,128)(2,1)S(1)} fusion(f32[1024,16]{0,1:T(8,128)S(1)} %all_gather.10, f32[1024,128]{1,0:T(8,128)} %gather_fusion.1, pred[1024]{0:T(1024)(128)(4,1)S(1)} %compare_and_fusion.2), kind=kOutput, calls=%fused_computation.37 | convolution fusion | flops 25298944 | bytes 594944 | tf_op jit(solution)/shard_map/dot_general | solution.py:64
  84.1 2.4 %fusion.14 = f32[80,128,16]{1,2,0:T(8,128)} fusion(bf16[1,1,80,128,128]{4,3,2,1,0:T(8,128)(2,1)S(1)} %copy-done, bf16[80,128,16]{1,2,0:T(8,128)(2,1)S(1)} %gather_fusion.5, pred[80]{0:T(512)(128)(4,1)S(1)} %copy-done.12), kind=kOutput, calls=%fused_computation.26 | convolution fusion | flops 42106880 | bytes 3604560 | tf_op jit(solution)/shard_map/tij,tjr->tir/dot_general | solution.py:75
  87.2 2.2 %fusion.25 = f32[10,128,16]{1,0,2:T(8,128)} fusion(f32[80,128,16]{1,2,0:T(8,128)} %fusion.14, s32[80]{0:T(128)S(1)} %copy-done.11), kind=kOutput, calls=%fused_computation.41 | convolution fusion | flops 19661600 | bytes 737600 | tf_op jit(solution)/shard_map/bt,tir->bir/dot_general | solution.py:78
  89.4 3.8 %collective-permute-start.10 = (f32[128,16]{0,1:T(8,128)S(1)}, f32[128,16]{0,1:T(8,128)S(1)}, u32[]{:S(2)}, u32[]{:S(2)}) collective-permute-start(f32[128,16]{0,1:T(8,128)S(1)} %get-tuple-element.19), channel_id=1, source_target_pairs={{0,3},{1,0},{2,1},{3,2},{4,7},{5,4},{6,5},{7,6},{8,11},{9,8},{10,9... | collective-permute-start | bytes 24584 | tf_op jit(solution)/shard_map/ppermute | solution.py:11
  93.2 3.8 %collective-permute-start.12 = (f32[128,16]{0,1:T(8,128)S(1)}, f32[128,16]{0,1:T(8,128)S(1)}, u32[]{:S(2)}, u32[]{:S(2)}) collective-permute-start(f32[128,16]{0,1:T(8,128)S(1)} %get-tuple-element.17), channel_id=1, source_target_pairs={{0,3},{1,0},{2,1},{3,2},{4,7},{5,4},{6,5},{7,6},{8,11},{9,8},{10,9... | collective-permute-start | bytes 24584 | tf_op jit(solution)/shard_map/ppermute | solution.py:11
  97.0 2.6 %collective-permute-start.14 = (f32[128,16]{0,1:T(8,128)S(1)}, f32[128,16]{0,1:T(8,128)S(1)}, u32[]{:S(2)}, u32[]{:S(2)}) collective-permute-start(f32[128,16]{0,1:T(8,128)S(1)} %get-tuple-element.15), channel_id=1, source_target_pairs={{0,28},{4,0},{8,4},{12,8},{16,12},{20,16},{24,20},{28,24},{1,29},{... | collective-permute-start | bytes 24584 | tf_op jit(solution)/shard_map/ppermute | solution.py:11
  99.7 1.3 collective-permute-done.13
  101.2 7.0 %gather_fusion.7 = f32[768,16]{1,0:T(8,128)} fusion(f32[6,128,16]{2,1,0:T(8,128)S(1)} %copy.40, s32[768]{0:T(1024)S(1)} %bitcast.251), kind=kCustom, calls=%fused_computation.7.clone | custom fusion | bytes 104448 | tf_op jit(solution)/shard_map/jit(take_along_axis)/gather | solution.py:87
  108.2 1.2 copy.41
  109.4 1.2 fusion.21
  110.8 9.3 %all_gather.11 = f32[1024,16]{0,1:T(8,128)S(1)} all-gather(f32[128,16]{0,1:T(8,128)S(1)} %convolution_bitcast_fusion.3), channel_id=1, replica_groups=mesh['sub'=8,'reg'=4] {'sub'}, dimensions={0}, use_global_device_ids=true | all-gather | bytes 73728 | tf_op jit(solution)/shard_map/all_gather | solution.py:66
  120.1 1.5 %convolution_convert_fusion = bf16[128,16]{0,1:T(8,128)(2,1)S(1)} fusion(f32[1024,16]{0,1:T(8,128)S(1)} %all_gather.11, f32[1024,128]{1,0:T(8,128)} %gather_fusion.1, pred[1024]{0:T(1024)(128)(4,1)S(1)} %compare_and_fusion.2), kind=kOutput, calls=%fused_computation.36 | convolution fusion | flops 25298944 | bytes 594944 | tf_op jit(solution)/shard_map/dot_general | solution.py:64
  123.3 2.4 %fusion.17 = f32[80,128,16]{1,2,0:T(8,128)} fusion(bf16[1,1,80,128,128]{4,3,2,1,0:T(8,128)(2,1)S(1)} %copy-done, bf16[80,128,16]{1,2,0:T(8,128)(2,1)S(1)} %gather_fusion.8, pred[80]{0:T(512)(128)(4,1)S(1)} %copy-done.12), kind=kOutput, calls=%fused_computation.27 | convolution fusion | flops 42106880 | bytes 3604560 | tf_op jit(solution)/shard_map/tij,tjr->tir/dot_general | solution.py:75
  126.4 2.2 %fusion.23 = f32[10,128,16]{1,0,2:T(8,128)} fusion(f32[80,128,16]{1,2,0:T(8,128)} %fusion.17, s32[80]{0:T(128)S(1)} %copy-done.11), kind=kOutput, calls=%fused_computation.39 | convolution fusion | flops 19661600 | bytes 737600 | tf_op jit(solution)/shard_map/bt,tir->bir/dot_general | solution.py:78
  128.6 3.8 %collective-permute-start.16 = (f32[128,16]{0,1:T(8,128)S(1)}, f32[128,16]{0,1:T(8,128)S(1)}, u32[]{:S(2)}, u32[]{:S(2)}) collective-permute-start(f32[128,16]{0,1:T(8,128)S(1)} %get-tuple-element.13), channel_id=1, source_target_pairs={{0,3},{1,0},{2,1},{3,2},{4,7},{5,4},{6,5},{7,6},{8,11},{9,8},{10,9... | collective-permute-start | bytes 24584 | tf_op jit(solution)/shard_map/ppermute | solution.py:11
  132.4 3.8 %collective-permute-start.18 = (f32[128,16]{0,1:T(8,128)S(1)}, f32[128,16]{0,1:T(8,128)S(1)}, u32[]{:S(2)}, u32[]{:S(2)}) collective-permute-start(f32[128,16]{0,1:T(8,128)S(1)} %get-tuple-element.11), channel_id=1, source_target_pairs={{0,3},{1,0},{2,1},{3,2},{4,7},{5,4},{6,5},{7,6},{8,11},{9,8},{10,9... | collective-permute-start | bytes 24584 | tf_op jit(solution)/shard_map/ppermute | solution.py:11
  136.2 2.6 %collective-permute-start.20 = (f32[128,16]{0,1:T(8,128)S(1)}, f32[128,16]{0,1:T(8,128)S(1)}, u32[]{:S(2)}, u32[]{:S(2)}) collective-permute-start(f32[128,16]{0,1:T(8,128)S(1)} %get-tuple-element.9), channel_id=1, source_target_pairs={{0,28},{4,0},{8,4},{12,8},{16,12},{20,16},{24,20},{28,24},{1,29},{... | collective-permute-start | bytes 24584 | tf_op jit(solution)/shard_map/ppermute | solution.py:11
  138.9 1.3 collective-permute-done.19
  140.4 5.1 %gather_fusion.10 = f32[768,16]{1,0:T(8,128)S(1)} fusion(f32[6,128,16]{2,1,0:T(8,128)S(1)} %copy.45, s32[768]{0:T(1024)S(1)} %bitcast.252), kind=kCustom, calls=%fused_computation.8.clone | custom fusion | bytes 104448 | tf_op jit(solution)/shard_map/jit(take_along_axis)/gather | solution.py:87
  145.7 1.2 fusion.20
  (114 shorter events, 13.7 us)
Async XLA Ops:
  0.6 48.1 %copy-start = (bf16[1,1,80,128,128]{4,3,2,1,0:T(8,128)(2,1)S(1)}, bf16[1,1,80,128,128]{4,3,2,1,0:T(8,128)(2,1)}, u32[]{:S(2)}) copy-start(bf16[1,1,80,128,128]{4,3,2,1,0:T(8,128)(2,1)} %param.16) | copy-start | bytes 7864324
  0.6 33.0 %copy-start.5 = (s32[1,1,6,128]{3,1,2,0:T(1,128)S(1)}, s32[1,1,6,128]{3,1,2,0:T(1,128)}, u32[]{:S(2)}) copy-start(s32[1,1,6,128]{3,1,2,0:T(1,128)} %param.20) | copy-start | bytes 9220
  0.7 33.0 %copy-start.6 = (f32[1,1,1280]{2,1,0:T(1,128)S(1)}, f32[1,1,1280]{2,1,0:T(1,128)}, u32[]{:S(2)}) copy-start(f32[1,1,1280]{2,1,0:T(1,128)} %param.18) | copy-start | bytes 15364
  0.7 6.3 %collective-permute-start = (s32[128]{0:T(128)}, s32[128]{0:T(128)S(1)}, u32[]{:S(2)}, u32[]{:S(2)}) collective-permute-start(s32[128]{0:T(128)} %bitcast.274), channel_id=1, source_target_pairs={{0,4},{4,0},{8,12},{12,8},{16,20},{20,16},{24,28},{28,24},{1,5},{5... | collective-permute-start | bytes 1544 | tf_op jit(solution)/shard_map/ppermute | solution.py:47
  5.0 35.1 %copy-start.8 = (pred[6]{0:T(512)(128)(4,1)}, pred[6]{0:T(512)(128)(4,1)S(1)}, u32[]{:S(2)}) copy-start(pred[6]{0:T(512)(128)(4,1)S(1)} %compare_and_fusion.3) | copy-start | bytes 22
  7.7 4.2 %collective-permute-start.1 = (s32[256]{0:T(256)S(1)}, s32[256]{0:T(256)S(1)}, u32[]{:S(2)}, u32[]{:S(2)}) collective-permute-start(s32[256]{0:T(256)S(1)} %add_select_fusion.4), channel_id=1, source_target_pairs={{0,8},{4,12},{8,0},{12,4},{16,24},{20,28},{24,16},{28,20},{1,9},{5... | collective-permute-start | bytes 3080 | tf_op jit(solution)/shard_map/ppermute | solution.py:47
  11.9 3.7 %collective-permute-start.2 = (s32[512]{0:T(512)S(1)}, s32[512]{0:T(512)S(1)}, u32[]{:S(2)}, u32[]{:S(2)}) collective-permute-start(s32[512]{0:T(512)S(1)} %add_select_fusion.2), channel_id=1, source_target_pairs={{0,16},{4,20},{8,24},{12,28},{16,0},{20,4},{24,8},{28,12},{1,17},{... | collective-permute-start | bytes 6152 | tf_op jit(solution)/shard_map/ppermute | solution.py:47
  19.3 14.4 %all-to-all-start = ((f32[64,8,128]{2,0,1:T(8,128)}), f32[64,8,128]{2,0,1:T(8,128)S(1)}, u32[]{:S(2)}, u32[]{:S(2)}) async-start(f32[64,8,128]{2,0,1:T(8,128)} %broadcast_select_fusion), calls=%async_computation | async-start | bytes 524288 | tf_op jit(solution)/shard_map/all_to_all | solution.py:56
  33.8 5.6 %copy-start.1 = (bf16[1,1,1280,128]{3,2,1,0:T(8,128)(2,1)S(1)}, bf16[1,1,1280,128]{3,2,1,0:T(8,128)(2,1)}, u32[]{:S(2)}) copy-start(bf16[1,1,1280,128]{3,2,1,0:T(8,128)(2,1)} %param.21) | copy-start | bytes 983044
  33.8 5.6 %copy-start.2 = (f32[1,1,1280,16]{2,3,1,0:T(8,128)S(1)}, f32[1,1,1280,16]{2,3,1,0:T(8,128)}, u32[]{:S(2)}) copy-start(f32[1,1,1280,16]{2,3,1,0:T(8,128)} %param.15) | copy-start | bytes 245764
  40.3 11.8 %collective-permute-start.3 = (f32[128,16]{0,1:T(8,128)S(1)}, f32[128,16]{0,1:T(8,128)}, u32[]{:S(2)}, u32[]{:S(2)}) collective-permute-start(f32[128,16]{0,1:T(8,128)S(1)} %get-tuple-element.26), channel_id=1, source_target_pairs={{0,1},{1,2},{2,3},{3,0},{4,5},{5,6},{6,7},{7,4},{8,9},{9,10},{10,1... | collective-permute-start | bytes 24584 | tf_op jit(solution)/shard_map/ppermute | solution.py:11
  41.9 14.2 %collective-permute-start.4 = (f32[128,16]{0,1:T(8,128)S(1)}, f32[128,16]{0,1:T(8,128)}, u32[]{:S(2)}, u32[]{:S(2)}) collective-permute-start(f32[128,16]{0,1:T(8,128)S(1)} %get-tuple-element.25), channel_id=1, source_target_pairs={{0,3},{1,0},{2,1},{3,2},{4,7},{5,4},{6,5},{7,6},{8,11},{9,8},{10,9... | collective-permute-start | bytes 24584 | tf_op jit(solution)/shard_map/ppermute | solution.py:11
  44.1 13.2 %collective-permute-start.5 = (f32[128,16]{0,1:T(8,128)S(1)}, f32[128,16]{0,1:T(8,128)}, u32[]{:S(2)}, u32[]{:S(2)}) collective-permute-start(f32[128,16]{0,1:T(8,128)S(1)} %get-tuple-element.24), channel_id=1, source_target_pairs={{0,1},{1,2},{2,3},{3,0},{4,5},{5,6},{6,7},{7,4},{8,9},{9,10},{10,1... | collective-permute-start | bytes 24584 | tf_op jit(solution)/shard_map/ppermute | solution.py:11
  44.1 14.5 %collective-permute-start.6 = (f32[128,16]{0,1:T(8,128)S(1)}, f32[128,16]{0,1:T(8,128)}, u32[]{:S(2)}, u32[]{:S(2)}) collective-permute-start(f32[128,16]{0,1:T(8,128)S(1)} %get-tuple-element.23), channel_id=1, source_target_pairs={{0,3},{1,0},{2,1},{3,2},{4,7},{5,4},{6,5},{7,6},{8,11},{9,8},{10,9... | collective-permute-start | bytes 24584 | tf_op jit(solution)/shard_map/ppermute | solution.py:11
  48.0 12.0 %collective-permute-start.7 = (f32[128,16]{0,1:T(8,128)S(1)}, f32[128,16]{0,1:T(8,128)}, u32[]{:S(2)}, u32[]{:S(2)}) collective-permute-start(f32[128,16]{0,1:T(8,128)S(1)} %get-tuple-element.22), channel_id=1, source_target_pairs={{0,4},{4,8},{8,12},{12,16},{16,20},{20,24},{24,28},{28,0},{1,5},{5... | collective-permute-start | bytes 24584 | tf_op jit(solution)/shard_map/ppermute | solution.py:11
  48.7 2.2 %copy-start.10 = (s32[80]{0:T(128)S(1)}, s32[80]{0:T(128)}, u32[]{:S(2)}) copy-start(s32[80]{0:T(128)} %slice_bitcast_fusion.18) | copy-start | bytes 964
  52.1 18.8 %copy-start.7 = (s32[1,1,6]{2,1,0:T(1,128)S(1)}, s32[1,1,6]{2,1,0:T(1,128)}, u32[]{:S(2)}) copy-start(s32[1,1,6]{2,1,0:T(1,128)} %param.19) | copy-start | bytes 76
  52.1 9.1 %collective-permute-start.8 = (f32[128,16]{0,1:T(8,128)S(1)}, f32[128,16]{0,1:T(8,128)S(1)}, u32[]{:S(2)}, u32[]{:S(2)}) collective-permute-start(f32[128,16]{0,1:T(8,128)S(1)} %get-tuple-element.21), channel_id=1, source_target_pairs={{0,28},{4,0},{8,4},{12,8},{16,12},{20,16},{24,20},{28,24},{1,29},{... | collective-permute-start | bytes 24584 | tf_op jit(solution)/shard_map/ppermute | solution.py:11
  82.5 0.6 copy-start.3
  83.1 0.9 copy-start.12
  84.1 3.0 %copy-start.9 = (pred[6]{0:T(512)(128)(4,1)S(1)}, pred[6]{0:T(512)(128)(4,1)}, u32[]{:S(2)}) copy-start(pred[6]{0:T(512)(128)(4,1)} %copy-done.8) | copy-start | bytes 22
  84.1 3.1 %copy-start.11 = (s32[80]{0:T(128)S(1)}, s32[80]{0:T(128)}, u32[]{:S(2)}) copy-start(s32[80]{0:T(128)} %slice_bitcast_fusion.18) | copy-start | bytes 964
  87.1 9.9 %collective-permute-start.9 = (f32[128,16]{0,1:T(8,128)S(1)}, f32[128,16]{0,1:T(8,128)S(1)}, u32[]{:S(2)}, u32[]{:S(2)}) collective-permute-start(f32[128,16]{0,1:T(8,128)S(1)} %get-tuple-element.20), channel_id=1, source_target_pairs={{0,1},{1,2},{2,3},{3,0},{4,5},{5,6},{6,7},{7,4},{8,9},{9,10},{10,1... | collective-permute-start | bytes 24584 | tf_op jit(solution)/shard_map/ppermute | solution.py:11
  89.4 10.3 %collective-permute-start.10 = (f32[128,16]{0,1:T(8,128)S(1)}, f32[128,16]{0,1:T(8,128)S(1)}, u32[]{:S(2)}, u32[]{:S(2)}) collective-permute-start(f32[128,16]{0,1:T(8,128)S(1)} %get-tuple-element.19), channel_id=1, source_target_pairs={{0,3},{1,0},{2,1},{3,2},{4,7},{5,4},{6,5},{7,6},{8,11},{9,8},{10,9... | collective-permute-start | bytes 24584 | tf_op jit(solution)/shard_map/ppermute | solution.py:11
  93.2 6.5 %collective-permute-start.11 = (f32[128,16]{0,1:T(8,128)S(1)}, f32[128,16]{0,1:T(8,128)S(1)}, u32[]{:S(2)}, u32[]{:S(2)}) collective-permute-start(f32[128,16]{0,1:T(8,128)S(1)} %get-tuple-element.18), channel_id=1, source_target_pairs={{0,1},{1,2},{2,3},{3,0},{4,5},{5,6},{6,7},{7,4},{8,9},{9,10},{10,1... | collective-permute-start | bytes 24584 | tf_op jit(solution)/shard_map/ppermute | solution.py:11
  93.2 6.5 %collective-permute-start.12 = (f32[128,16]{0,1:T(8,128)S(1)}, f32[128,16]{0,1:T(8,128)S(1)}, u32[]{:S(2)}, u32[]{:S(2)}) collective-permute-start(f32[128,16]{0,1:T(8,128)S(1)} %get-tuple-element.17), channel_id=1, source_target_pairs={{0,3},{1,0},{2,1},{3,2},{4,7},{5,4},{6,5},{7,6},{8,11},{9,8},{10,9... | collective-permute-start | bytes 24584 | tf_op jit(solution)/shard_map/ppermute | solution.py:11
  97.0 4.0 %collective-permute-start.13 = (f32[128,16]{0,1:T(8,128)S(1)}, f32[128,16]{0,1:T(8,128)S(1)}, u32[]{:S(2)}, u32[]{:S(2)}) collective-permute-start(f32[128,16]{0,1:T(8,128)S(1)} %get-tuple-element.16), channel_id=1, source_target_pairs={{0,4},{4,8},{8,12},{12,16},{16,20},{20,24},{24,28},{28,0},{1,5},{5... | collective-permute-start | bytes 24584 | tf_op jit(solution)/shard_map/ppermute | solution.py:11
  97.0 4.0 %collective-permute-start.14 = (f32[128,16]{0,1:T(8,128)S(1)}, f32[128,16]{0,1:T(8,128)S(1)}, u32[]{:S(2)}, u32[]{:S(2)}) collective-permute-start(f32[128,16]{0,1:T(8,128)S(1)} %get-tuple-element.15), channel_id=1, source_target_pairs={{0,28},{4,0},{8,4},{12,8},{16,12},{20,16},{24,20},{28,24},{1,29},{... | collective-permute-start | bytes 24584 | tf_op jit(solution)/shard_map/ppermute | solution.py:11
  101.2 20.4 %copy-start.4 = (f32[1280,16]{0,1:T(8,128)S(1)}, f32[1280,16]{0,1:T(8,128)}, u32[]{:S(2)}) copy-start(f32[1280,16]{0,1:T(8,128)} %copy-done.3) | copy-start | bytes 245764
  126.3 9.9 %collective-permute-start.15 = (f32[128,16]{0,1:T(8,128)S(1)}, f32[128,16]{0,1:T(8,128)S(1)}, u32[]{:S(2)}, u32[]{:S(2)}) collective-permute-start(f32[128,16]{0,1:T(8,128)S(1)} %get-tuple-element.14), channel_id=1, source_target_pairs={{0,1},{1,2},{2,3},{3,0},{4,5},{5,6},{6,7},{7,4},{8,9},{9,10},{10,1... | collective-permute-start | bytes 24584 | tf_op jit(solution)/shard_map/ppermute | solution.py:11
  128.6 10.3 %collective-permute-start.16 = (f32[128,16]{0,1:T(8,128)S(1)}, f32[128,16]{0,1:T(8,128)S(1)}, u32[]{:S(2)}, u32[]{:S(2)}) collective-permute-start(f32[128,16]{0,1:T(8,128)S(1)} %get-tuple-element.13), channel_id=1, source_target_pairs={{0,3},{1,0},{2,1},{3,2},{4,7},{5,4},{6,5},{7,6},{8,11},{9,8},{10,9... | collective-permute-start | bytes 24584 | tf_op jit(solution)/shard_map/ppermute | solution.py:11
  132.4 6.5 %collective-permute-start.17 = (f32[128,16]{0,1:T(8,128)S(1)}, f32[128,16]{0,1:T(8,128)S(1)}, u32[]{:S(2)}, u32[]{:S(2)}) collective-permute-start(f32[128,16]{0,1:T(8,128)S(1)} %get-tuple-element.12), channel_id=1, source_target_pairs={{0,1},{1,2},{2,3},{3,0},{4,5},{5,6},{6,7},{7,4},{8,9},{9,10},{10,1... | collective-permute-start | bytes 24584 | tf_op jit(solution)/shard_map/ppermute | solution.py:11
  132.4 6.5 %collective-permute-start.18 = (f32[128,16]{0,1:T(8,128)S(1)}, f32[128,16]{0,1:T(8,128)S(1)}, u32[]{:S(2)}, u32[]{:S(2)}) collective-permute-start(f32[128,16]{0,1:T(8,128)S(1)} %get-tuple-element.11), channel_id=1, source_target_pairs={{0,3},{1,0},{2,1},{3,2},{4,7},{5,4},{6,5},{7,6},{8,11},{9,8},{10,9... | collective-permute-start | bytes 24584 | tf_op jit(solution)/shard_map/ppermute | solution.py:11
  136.2 4.0 %collective-permute-start.19 = (f32[128,16]{0,1:T(8,128)S(1)}, f32[128,16]{0,1:T(8,128)S(1)}, u32[]{:S(2)}, u32[]{:S(2)}) collective-permute-start(f32[128,16]{0,1:T(8,128)S(1)} %get-tuple-element.10), channel_id=1, source_target_pairs={{0,4},{4,8},{8,12},{12,16},{16,20},{20,24},{24,28},{28,0},{1,5},{5... | collective-permute-start | bytes 24584 | tf_op jit(solution)/shard_map/ppermute | solution.py:11
  136.2 4.0 %collective-permute-start.20 = (f32[128,16]{0,1:T(8,128)S(1)}, f32[128,16]{0,1:T(8,128)S(1)}, u32[]{:S(2)}, u32[]{:S(2)}) collective-permute-start(f32[128,16]{0,1:T(8,128)S(1)} %get-tuple-element.9), channel_id=1, source_target_pairs={{0,28},{4,0},{8,4},{12,8},{16,12},{20,16},{24,20},{28,24},{1,29},{... | collective-permute-start | bytes 24584 | tf_op jit(solution)/shard_map/ppermute | solution.py:11
